TPU v7x, 32 devices: a whole 2x2x4 slice. The times are simulated.
32 devices in a mesh: dp: 4 (over x, core), cls: 8 (over z, y).
Axes of the slice: x: 2, y: 2, z: 4, core: 2. Of those that a mesh axis runs over, the one named last changes fastest.
Arguments:
- pooled: bfloat16 [4096, 512], P(('dp', 'cls')), may hold values from -6 to 6
- proj: bfloat16 [512, 512], replicated, may hold values from -0.25 to 0.25
- centers: bfloat16 [2048, 512], P('cls'), may hold values from -6 to 6
- labels: int32 [4096], P(('dp', 'cls')), may hold values from 0 to 2047
- row_weight: bfloat16 [4096], P(('dp', 'cls')), may hold values from 0.5 to 2
Outputs:
- row_loss: float32 [4096], P(('dp', 'cls'))
- center_grad: float32 [2048, 512], P('cls')
- proj_grad: float32 [512, 512], replicated
All inputs are finite; a program needn't handle non-finite values.
Results may differ from a plain program's by a relative error of at most 0.005.
Values may be sent and summed in bfloat16 or wider, within the bound.
No kernel may reach another device: no remote copies, remote signals or barrier semaphores. Data moves between devices by JAX's collectives and lax.ppermute only.
A program may use at most 128 MiB of HBM per device.

v0:
```python
import math

import jax
import jax.numpy as jnp
from jax import lax
from jax.sharding import PartitionSpec as P


SCALE = 64.0
MARGIN = 0.35
EPS = 1e-06
F32 = jnp.float32
BF16 = jnp.bfloat16


def unit_rows(values):
    inverse = lax.rsqrt(jnp.sum(values * values, axis=1, keepdims=True) + EPS)
    return ((values * inverse).astype(BF16), inverse)


def size_of(axes):
    return math.prod(lax.axis_size(a) for a in axes)


def swap(x, axes, mask):
    return lax.ppermute(x, axes, [(i, i ^ mask) for i in range(size_of(axes))])


def dot(a, b, ca, cb):
    return lax.dot_general(a, b, (((ca,), (cb,)), ((), ())), preferred_element_type=F32)


def scatter_sum(x, axes):
    size = size_of(axes)
    if size == 1:
        return x
    index = lax.axis_index(axes)
    rows = x.shape[0] // size
    total = lax.dynamic_slice_in_dim(x, index * rows, rows)
    sent = [lax.dynamic_slice_in_dim(x, (index ^ mask) * rows, rows).astype(BF16) for mask in range(1, size)]
    parts = [swap(out, axes, mask) for mask, out in enumerate(sent, 1)]
    for part in parts:
        total = total + part.astype(F32)
    return total


def full_sum(x, axes):
    groups = [axes] if size_of(axes) <= 4 else [(a,) for a in axes]
    for group in groups:
        size = size_of(group)
        sent = x.astype(BF16)
        parts = [sent] + [swap(sent, group, mask) for mask in range(1, size)]
        span = size
        while span > 1:
            parts = [parts[i].astype(F32) + parts[i + span // 2].astype(F32) for i in range(span // 2)]
            span //= 2
        x = parts[0]
    return x


def gather_rows(x, axes):
    size = size_of(axes)
    if size == 1:
        return x
    index = lax.axis_index(axes)
    full = jnp.zeros((size * x.shape[0],) + x.shape[1:], x.dtype)
    full = lax.dynamic_update_slice_in_dim(full, x, index * x.shape[0], 0)
    for mask in range(1, size):
        part = swap(x, axes, mask)
        full = lax.dynamic_update_slice_in_dim(full, part, (index ^ mask) * x.shape[0], 0)
    return full


def on_device(pooled, proj, centers, labels, row_weight):
    s_axes = ("sz", "sy")
    ns, nk, nl = size_of(s_axes), size_of(("k",)), size_of(("dl",))
    rows, _ = pooled.shape
    c_dev = centers.shape[0]
    half = c_dev // nl
    at_s, at_k, at_l = (lax.axis_index(a) for a in (s_axes, "k", "dl"))
    mine = lax.optimization_barrier(lax.dynamic_slice_in_dim(centers, at_l * half, half))
    own_parts = [mine] + [swap(mine, ("k",), j) for j in range(1, nk)]
    blocks = [pooled] + [swap(pooled, s_axes, m) for m in range(1, ns)]
    meta = lax.optimization_barrier(jnp.concatenate([labels.astype(F32), row_weight.astype(F32)]).reshape(1, 2 * rows))
    metas = [meta] + [swap(meta, s_axes, m) for m in range(1, ns)]
    label_of = [m[:, :rows].astype(jnp.int32) for m in metas]
    weights = [m[:, rows:] for m in metas]
    cents = list(own_parts)
    for c in range(1, nl):
        cents.append(lax.dynamic_slice_in_dim(centers, (at_l ^ c) * half, half))
        cents += [swap(own_parts[j], ("dl",), c) for j in range(1, nk)]
    pairs = [unit_rows(part.astype(F32)) for part in cents]
    unit = jnp.concatenate([p[0] for p in pairs], axis=0)
    c_inv = pairs[0][1]
    label_all = jnp.concatenate(label_of, axis=1)
    weight_all = jnp.concatenate(weights, axis=1)
    local = lax.broadcasted_iota(jnp.int32, (half, 1), 0)
    ids = jnp.concatenate(
        [local + ((at_k ^ j) * ns + at_s) * c_dev + (at_l ^ c) * half for c in range(nl) for j in range(nk)], axis=0
    )
    embs, z_invs, expos, stats = [], [], [], []
    for m in range(ns):
        emb, z_inv = unit_rows(dot(blocks[m], proj, 1, 0))
        onehot = (ids == label_of[m]).astype(F32)
        logits = SCALE * dot(unit, emb, 1, 1) - SCALE * MARGIN * onehot
        expo = jnp.exp(logits)
        stats.append((jnp.sum(expo, axis=0, keepdims=True), jnp.sum(logits * onehot, axis=0, keepdims=True)))
        embs.append(emb)
        z_invs.append(z_inv)
        expos.append(expo)
    stats = jnp.concatenate([s[0] for s in stats] + [s[1] for s in stats], axis=1)
    total, target = stats[:, : ns * rows], stats[:, ns * rows : ns * rows + rows]
    for m in range(1, ns):
        other = swap(stats, s_axes, m)
        total = total + jnp.concatenate([other[:, (b ^ m) * rows : ((b ^ m) + 1) * rows] for b in range(ns)], axis=1)
        target = target + other[:, (ns + m) * rows : (ns + m + 1) * rows]
    row_loss = (jnp.log(total[:, :rows]) - target).reshape(rows)
    feats, emb, z_inv = (jnp.concatenate(x, axis=0) for x in (blocks, embs, z_invs))
    expo = jnp.concatenate(expos, axis=1)
    onehot = (ids == label_all).astype(F32)
    grad = (weight_all * (expo / total - onehot)).astype(BF16)
    grad_emb = SCALE * dot(grad, unit, 0, 0)
    emb_f = emb.astype(F32)
    grad_hidden = (z_inv * (grad_emb - emb_f * jnp.sum(emb_f * grad_emb, axis=1, keepdims=True))).astype(BF16)

    span = nk * half
    own = SCALE * dot(grad[:span], emb, 1, 0)
    for c in range(1, nl):
        send = (SCALE * dot(grad[c * span : (c + 1) * span], emb, 1, 0)).astype(BF16)
        own = own + swap(send, ("dl",), c).astype(F32)
    summed = own[:half]
    for j in range(1, nk):
        summed = summed + swap(own[j * half : (j + 1) * half].astype(BF16), ("k",), j).astype(F32)
    summed = full_sum(summed, ("dh",))
    unit_f = unit[:half].astype(F32)
    center_part = c_inv * (summed - unit_f * jnp.sum(unit_f * summed, axis=1, keepdims=True))
    center_grad = gather_rows(center_part, ("dl",))
    first, second = ("dh", "sy"), ("k", "sz")
    cols = feats.shape[1] // nl
    sends = [dot(lax.dynamic_slice_in_dim(feats, (at_l ^ c) * cols, cols, 1), grad_hidden, 0, 0).astype(BF16) for c in range(1, nl)]
    piece = dot(lax.dynamic_slice_in_dim(feats, at_l * cols, cols, 1), grad_hidden, 0, 0)
    piece = lax.optimization_barrier(piece)
    for c in range(1, nl):
        piece = piece + swap(sends[c - 1], ("dl",), c).astype(F32)
    piece = scatter_sum(piece, first)
    piece = full_sum(piece, second)
    piece = piece.astype(BF16)
    proj_grad = gather_rows(gather_rows(piece, first), ("dl",)).astype(F32)

    return (row_loss, center_grad, proj_grad)


def solution(mesh):
    dp, cls = mesh.shape["dp"], mesh.shape["cls"]
    nl = 2 if dp % 2 == 0 else 1
    bits = cls.bit_length() - 1
    ns = 1 << ((bits + 1) // 2)
    sy = min(2, ns)
    fine = jax.sharding.Mesh(
        mesh.devices.reshape(dp // nl, nl, cls // ns, ns // sy, sy), ("dh", "dl", "k", "sz", "sy")
    )
    dp_axes, cls_axes = ("dh", "dl"), ("k", "sz", "sy")
    every = dp_axes + cls_axes
    in_specs = (P(every, None), P(), P(cls_axes, None), P(every), P(every))
    out_specs = (P(every), P(cls_axes, None), P())

    return jax.shard_map(on_device, mesh=fine, in_specs=in_specs, out_specs=out_specs, check_vma=False)
```

profile of v0, /device:TPU:0, one launch (start us, length us, event | category | flops | bytes accessed | tf_op | source)
XLA Modules:
  0.0 65.7 jit_solution(737728805859922974)
XLA Ops:
  0.6 3.1 %collective-permute-start.2 = (bf16[128,512]{1,0:T(8,128)(2,1)}, bf16[128,512]{1,0:T(8,128)(2,1)S(1)}, u32[]{:S(2)}, u32[]{:S(2)}) collective-permute-start(bf16[128,512]{1,0:T(8,128)(2,1)} %param.5), channel_id=1, source_target_pairs={{0,1},{1,0},{2,3},{3,2},{4,5},{5,4},{6,7},{7,6},{8,9},{9,8},{10,11... | collective-permute-start | bytes 393224 | tf_op jit(solution)/shard_map/ppermute | solution.py:26
  3.7 1.5 %collective-permute-start.6 = (bf16[128,512]{1,0:T(8,128)(2,1)}, bf16[128,512]{1,0:T(8,128)(2,1)S(1)}, u32[]{:S(2)}, u32[]{:S(2)}) collective-permute-start(bf16[128,512]{1,0:T(8,128)(2,1)} %param.5), channel_id=1, source_target_pairs={{0,3},{1,2},{2,1},{3,0},{4,7},{5,6},{6,5},{7,4},{8,11},{9,10},{10,... | collective-permute-start | bytes 393224 | tf_op jit(solution)/shard_map/ppermute | solution.py:26
  5.3 0.9 %constant_dynamic-slice_fusion = bf16[128,512]{1,0:T(8,128)(2,1)S(1)} fusion(bf16[256,512]{1,0:T(8,128)(2,1)} %param.7, s32[]{:T(128)S(6)} %select_n.32), kind=kLoop, calls=%fused_computation.104 | loop fusion | bytes 262148 | tf_op jit(solution)/shard_map/dynamic_slice | solution.py:81
  6.3 3.0 %collective-permute-start = (bf16[128,512]{1,0:T(8,128)(2,1)S(1)}, bf16[128,512]{1,0:T(8,128)(2,1)S(1)}, u32[]{:S(2)}, u32[]{:S(2)}) collective-permute-start(bf16[128,512]{1,0:T(8,128)(2,1)S(1)} %constant_dynamic-slice_fusion), channel_id=1, source_target_pairs={{0,4},{4,0},{1,5},{5,1},{2,6},{6,2},{3,7},{7,3},{8,12},{12,8},{9,1... | collective-permute-start | bytes 393224 | tf_op jit(solution)/shard_map/ppermute | solution.py:26
  9.3 1.6 %collective-permute-start.3 = (f32[1,256]{1,0:T(1,128)S(1)}, f32[1,256]{1,0:T(1,128)S(1)}, u32[]{:S(2)}, u32[]{:S(2)}) collective-permute-start(f32[1,256]{1,0:T(1,128)S(1)} %bitcast.85), channel_id=1, source_target_pairs={{0,1},{1,0},{2,3},{3,2},{4,5},{5,4},{6,7},{7,6},{8,9},{9,8},{10,11... | collective-permute-start | bytes 3080 | tf_op jit(solution)/shard_map/ppermute | solution.py:26
  11.7 1.3 %collective-permute-done.3 = f32[1,256]{1,0:T(1,128)S(1)} collective-permute-done((f32[1,256]{1,0:T(1,128)S(1)}, f32[1,256]{1,0:T(1,128)S(1)}, u32[]{:S(2)}, u32[]{:S(2)}) %collective-permute-start.3) | collective-permute-done | bytes 1056 | tf_op jit(solution)/shard_map/ppermute | solution.py:26
  13.0 1.6 %collective-permute-start.5 = (f32[1,256]{1,0:T(1,128)S(1)}, f32[1,256]{1,0:T(1,128)S(1)}, u32[]{:S(2)}, u32[]{:S(2)}) collective-permute-start(f32[1,256]{1,0:T(1,128)S(1)} %bitcast.87), channel_id=1, source_target_pairs={{0,2},{1,3},{2,0},{3,1},{4,6},{5,7},{6,4},{7,5},{8,10},{9,11},{10,... | collective-permute-start | bytes 3080 | tf_op jit(solution)/shard_map/ppermute | solution.py:26
  14.6 2.0 %collective-permute-done.5 = f32[1,256]{1,0:T(1,128)S(1)} collective-permute-done((f32[1,256]{1,0:T(1,128)S(1)}, f32[1,256]{1,0:T(1,128)S(1)}, u32[]{:S(2)}, u32[]{:S(2)}) %collective-permute-start.5) | collective-permute-done | bytes 1056 | tf_op jit(solution)/shard_map/ppermute | solution.py:26
  16.5 2.5 %collective-permute-start.7 = (f32[1,256]{1,0:T(1,128)S(1)}, f32[1,256]{1,0:T(1,128)S(1)}, u32[]{:S(2)}, u32[]{:S(2)}) collective-permute-start(f32[1,256]{1,0:T(1,128)S(1)} %bitcast.88), channel_id=1, source_target_pairs={{0,3},{1,2},{2,1},{3,0},{4,7},{5,6},{6,5},{7,4},{8,11},{9,10},{10,... | collective-permute-start | bytes 3080 | tf_op jit(solution)/shard_map/ppermute | solution.py:26
  19.1 1.9 %collective-permute-done.7 = f32[1,256]{1,0:T(1,128)S(1)} collective-permute-done((f32[1,256]{1,0:T(1,128)S(1)}, f32[1,256]{1,0:T(1,128)S(1)}, u32[]{:S(2)}, u32[]{:S(2)}) %collective-permute-start.7) | collective-permute-done | bytes 1056 | tf_op jit(solution)/shard_map/ppermute | solution.py:26
  22.8 1.2 %collective-permute-done.1 = bf16[128,512]{1,0:T(8,128)(2,1)S(1)} collective-permute-done((bf16[128,512]{1,0:T(8,128)(2,1)S(1)}, bf16[128,512]{1,0:T(8,128)(2,1)S(1)}, u32[]{:S(2)}, u32[]{:S(2)}) %collective-permute-start.1) | collective-permute-done | bytes 131104 | tf_op jit(solution)/shard_map/ppermute | solution.py:26
  25.6 2.6 %collective-permute-start.10 = (f32[1,1024]{1,0:T(1,128)S(1)}, f32[1,1024]{1,0:T(1,128)S(1)}, u32[]{:S(2)}, u32[]{:S(2)}) collective-permute-start(f32[1,1024]{1,0:T(1,128)S(1)} %constant_dynamic-update-slice_fusion), channel_id=1, source_target_pairs={{0,3},{1,2},{2,1},{3,0},{4,7},{5,6},{6,5},{7,4},{8,11},{9,10},{10,... | collective-permute-start | bytes 12296 | tf_op jit(solution)/shard_map/ppermute | solution.py:26
  29.2 1.0 %collective-permute-done.10 = f32[1,1024]{1,0:T(1,128)S(1)} collective-permute-done((f32[1,1024]{1,0:T(1,128)S(1)}, f32[1,1024]{1,0:T(1,128)S(1)}, u32[]{:S(2)}, u32[]{:S(2)}) %collective-permute-start.10) | collective-permute-done | bytes 4128 | tf_op jit(solution)/shard_map/ppermute | solution.py:26
  30.2 1.6 %collective-permute-done.8 = f32[1,1024]{1,0:T(1,128)S(1)} collective-permute-done((f32[1,1024]{1,0:T(1,128)S(1)}, f32[1,1024]{1,0:T(1,128)S(1)}, u32[]{:S(2)}, u32[]{:S(2)}) %collective-permute-start.8) | collective-permute-done | bytes 4128 | tf_op jit(solution)/shard_map/ppermute | solution.py:26
  32.6 0.6 fusion.5
  34.2 1.2 %collective-permute-done.15 = bf16[256,512]{1,0:T(8,128)(2,1)S(1)} collective-permute-done((bf16[256,512]{1,0:T(8,128)(2,1)S(1)}, bf16[256,512]{1,0:T(8,128)(2,1)S(1)}, u32[]{:S(2)}, u32[]{:S(2)}) %collective-permute-start.15) | collective-permute-done | bytes 262176 | tf_op jit(solution)/shard_map/ppermute | solution.py:26
  35.5 1.6 %collective-permute-start.16 = (bf16[64,512]{1,0:T(8,128)(2,1)S(1)}, bf16[64,512]{1,0:T(8,128)(2,1)S(1)}, u32[]{:S(2)}, u32[]{:S(2)}) collective-permute-start(bf16[64,512]{1,0:T(8,128)(2,1)S(1)} %get-tuple-element.21), channel_id=1, source_target_pairs={{0,1},{1,0},{16,17},{17,16},{2,3},{3,2},{18,19},{19,18},{4,5},{5,4... | collective-permute-start | bytes 196616 | tf_op jit(solution)/shard_map/ppermute | solution.py:26
  37.1 1.5 %collective-permute-start.17 = (bf16[64,512]{1,0:T(8,128)(2,1)S(1)}, bf16[64,512]{1,0:T(8,128)(2,1)S(1)}, u32[]{:S(2)}, u32[]{:S(2)}) collective-permute-start(bf16[64,512]{1,0:T(8,128)(2,1)S(1)} %get-tuple-element.23), channel_id=1, source_target_pairs={{0,16},{1,17},{16,0},{17,1},{2,18},{3,19},{18,2},{19,3},{4,20},{5,... | collective-permute-start | bytes 196616 | tf_op jit(solution)/shard_map/ppermute | solution.py:26
  39.8 2.2 %collective-permute-done.17 = bf16[64,512]{1,0:T(8,128)(2,1)S(1)} collective-permute-done((bf16[64,512]{1,0:T(8,128)(2,1)S(1)}, bf16[64,512]{1,0:T(8,128)(2,1)S(1)}, u32[]{:S(2)}, u32[]{:S(2)}) %collective-permute-start.17) | collective-permute-done | bytes 65568 | tf_op jit(solution)/shard_map/ppermute | solution.py:26
  42.0 1.7 %collective-permute-done.18 = bf16[64,512]{1,0:T(8,128)(2,1)S(1)} collective-permute-done((bf16[64,512]{1,0:T(8,128)(2,1)S(1)}, bf16[64,512]{1,0:T(8,128)(2,1)S(1)}, u32[]{:S(2)}, u32[]{:S(2)}) %collective-permute-start.18) | collective-permute-done | bytes 65568 | tf_op jit(solution)/shard_map/ppermute | solution.py:26
  44.2 0.6 collective-permute-start.20
  44.8 3.4 %collective-permute-start.21 = (bf16[64,512]{1,0:T(8,128)(2,1)S(1)}, bf16[64,512]{1,0:T(8,128)(2,1)S(1)}, u32[]{:S(2)}, u32[]{:S(2)}) collective-permute-start(bf16[64,512]{1,0:T(8,128)(2,1)S(1)} %add_convert_fusion.1), channel_id=1, source_target_pairs={{0,6},{2,4},{4,2},{6,0},{1,7},{3,5},{5,3},{7,1},{8,14},{10,12},{12... | collective-permute-start | bytes 196616 | tf_op jit(solution)/shard_map/ppermute | solution.py:26
  48.6 5.4 %collective-permute-done.19 = bf16[64,512]{1,0:T(8,128)(2,1)S(1)} collective-permute-done((bf16[64,512]{1,0:T(8,128)(2,1)S(1)}, bf16[64,512]{1,0:T(8,128)(2,1)S(1)}, u32[]{:S(2)}, u32[]{:S(2)}) %collective-permute-start.19) | collective-permute-done | bytes 65568 | tf_op jit(solution)/shard_map/ppermute | solution.py:26
  54.1 1.0 %collective-permute-start.22 = (bf16[64,512]{1,0:T(8,128)(2,1)S(1)}, bf16[64,512]{1,0:T(8,128)(2,1)S(1)}, u32[]{:S(2)}, u32[]{:S(2)}) collective-permute-start(bf16[64,512]{1,0:T(8,128)(2,1)S(1)} %get-tuple-element.18), channel_id=1, source_target_pairs={{0,1},{1,0},{16,17},{17,16},{2,3},{3,2},{18,19},{19,18},{4,5},{5,4... | collective-permute-start | bytes 196616 | tf_op jit(solution)/shard_map/ppermute | solution.py:26
  55.2 0.9 %collective-permute-start.23 = (bf16[64,512]{1,0:T(8,128)(2,1)S(1)}, bf16[64,512]{1,0:T(8,128)(2,1)S(1)}, u32[]{:S(2)}, u32[]{:S(2)}) collective-permute-start(bf16[64,512]{1,0:T(8,128)(2,1)S(1)} %get-tuple-element.18), channel_id=1, source_target_pairs={{0,16},{1,17},{16,0},{17,1},{2,18},{3,19},{18,2},{19,3},{4,20},{5,... | collective-permute-start | bytes 196616 | tf_op jit(solution)/shard_map/ppermute | solution.py:26
  56.0 1.7 %collective-permute-start.24 = (bf16[64,512]{1,0:T(8,128)(2,1)S(1)}, bf16[64,512]{1,0:T(8,128)(2,1)S(1)}, u32[]{:S(2)}, u32[]{:S(2)}) collective-permute-start(bf16[64,512]{1,0:T(8,128)(2,1)S(1)} %get-tuple-element.18), channel_id=1, source_target_pairs={{0,17},{1,16},{16,1},{17,0},{2,19},{3,18},{18,3},{19,2},{4,21},{5,... | collective-permute-start | bytes 196616 | tf_op jit(solution)/shard_map/ppermute | solution.py:26
  57.7 1.0 %collective-permute-start.13 = (bf16[128,512]{1,0:T(8,128)(2,1)S(1)}, bf16[128,512]{1,0:T(8,128)(2,1)S(1)}, u32[]{:S(2)}, u32[]{:S(2)}) collective-permute-start(bf16[128,512]{1,0:T(8,128)(2,1)S(1)} %fusion.27), channel_id=1, source_target_pairs={{0,16},{16,0},{1,17},{17,1},{2,18},{18,2},{3,19},{19,3},{4,20},{20... | collective-permute-start | bytes 393224 | tf_op jit(solution)/shard_map/ppermute | solution.py:26
  58.8 1.4 %collective-permute-done.23 = bf16[64,512]{1,0:T(8,128)(2,1)S(1)} collective-permute-done((bf16[64,512]{1,0:T(8,128)(2,1)S(1)}, bf16[64,512]{1,0:T(8,128)(2,1)S(1)}, u32[]{:S(2)}, u32[]{:S(2)}) %collective-permute-start.23) | collective-permute-done | bytes 65568 | tf_op jit(solution)/shard_map/ppermute | solution.py:26
  60.1 1.8 %collective-permute-done.24 = bf16[64,512]{1,0:T(8,128)(2,1)S(1)} collective-permute-done((bf16[64,512]{1,0:T(8,128)(2,1)S(1)}, bf16[64,512]{1,0:T(8,128)(2,1)S(1)}, u32[]{:S(2)}, u32[]{:S(2)}) %collective-permute-start.24) | collective-permute-done | bytes 65568 | tf_op jit(solution)/shard_map/ppermute | solution.py:26
  62.0 0.8 %collective-permute-done.13 = bf16[128,512]{1,0:T(8,128)(2,1)S(1)} collective-permute-done((bf16[128,512]{1,0:T(8,128)(2,1)S(1)}, bf16[128,512]{1,0:T(8,128)(2,1)S(1)}, u32[]{:S(2)}, u32[]{:S(2)}) %collective-permute-start.13) | collective-permute-done | bytes 131104 | tf_op jit(solution)/shard_map/ppermute | solution.py:26
  63.8 1.1 %convert_element_type.180 = f32[512,512]{1,0:T(8,128)} convert(bf16[512,512]{1,0:T(8,128)(2,1)S(1)} %constant_dynamic-update-slice_fusion.12) | non-fusion elementwise | flops 262144 | bytes 1572864 | tf_op jit(solution)/shard_map/convert_element_type | solution.py:148
  65.0 0.8 %copy-done.3 = f32[256,512]{1,0:T(8,128)} copy-done((f32[256,512]{1,0:T(8,128)}, f32[256,512]{1,0:T(8,128)S(1)}, u32[]{:S(2)}) %copy-start.3) | copy-done | bytes 524312
  (113 shorter events, 10.1 us)
Async XLA Ops:
  0.6 10.6 %copy-start = (bf16[512,512]{1,0:T(8,128)(2,1)S(1)}, bf16[512,512]{1,0:T(8,128)(2,1)}, u32[]{:S(2)}) copy-start(bf16[512,512]{1,0:T(8,128)(2,1)} %param.6) | copy-start | bytes 1572868
  0.6 20.4 %collective-permute-start.2 = (bf16[128,512]{1,0:T(8,128)(2,1)}, bf16[128,512]{1,0:T(8,128)(2,1)S(1)}, u32[]{:S(2)}, u32[]{:S(2)}) collective-permute-start(bf16[128,512]{1,0:T(8,128)(2,1)} %param.5), channel_id=1, source_target_pairs={{0,1},{1,0},{2,3},{3,2},{4,5},{5,4},{6,7},{7,6},{8,9},{9,8},{10,11... | collective-permute-start | bytes 393224 | tf_op jit(solution)/shard_map/ppermute | solution.py:26
  3.7 18.0 %collective-permute-start.6 = (bf16[128,512]{1,0:T(8,128)(2,1)}, bf16[128,512]{1,0:T(8,128)(2,1)S(1)}, u32[]{:S(2)}, u32[]{:S(2)}) collective-permute-start(bf16[128,512]{1,0:T(8,128)(2,1)} %param.5), channel_id=1, source_target_pairs={{0,3},{1,2},{2,1},{3,0},{4,7},{5,6},{6,5},{7,4},{8,11},{9,10},{10,... | collective-permute-start | bytes 393224 | tf_op jit(solution)/shard_map/ppermute | solution.py:26
  5.2 16.8 %collective-permute-start.4 = (bf16[128,512]{1,0:T(8,128)(2,1)}, bf16[128,512]{1,0:T(8,128)(2,1)S(1)}, u32[]{:S(2)}, u32[]{:S(2)}) collective-permute-start(bf16[128,512]{1,0:T(8,128)(2,1)} %param.5), channel_id=1, source_target_pairs={{0,2},{1,3},{2,0},{3,1},{4,6},{5,7},{6,4},{7,5},{8,10},{9,11},{10,... | collective-permute-start | bytes 393224 | tf_op jit(solution)/shard_map/ppermute | solution.py:26
  5.3 4.0 %copy-start.4 = (s32[128]{0:T(128)S(1)}, s32[128]{0:T(128)}, u32[]{:S(2)}) copy-start(s32[128]{0:T(128)} %param.8) | copy-start | bytes 1540
  5.3 4.0 %copy-start.5 = (bf16[128]{0:T(256)(128)(2,1)S(1)}, bf16[128]{0:T(256)(128)(2,1)}, u32[]{:S(2)}) copy-start(bf16[128]{0:T(256)(128)(2,1)} %param.9) | copy-start | bytes 772
  5.3 5.8 %copy-start.2 = (bf16[128,512]{1,0:T(8,128)(2,1)S(1)}, bf16[128,512]{1,0:T(8,128)(2,1)}, u32[]{:S(2)}) copy-start(bf16[128,512]{1,0:T(8,128)(2,1)} %param.5) | copy-start | bytes 393220
  6.2 4.8 %copy-start.1 = (bf16[256,512]{1,0:T(8,128)(2,1)S(1)}, bf16[256,512]{1,0:T(8,128)(2,1)}, u32[]{:S(2)}) copy-start(bf16[256,512]{1,0:T(8,128)(2,1)} %param.7) | copy-start | bytes 786436
  6.3 15.3 %collective-permute-start = (bf16[128,512]{1,0:T(8,128)(2,1)S(1)}, bf16[128,512]{1,0:T(8,128)(2,1)S(1)}, u32[]{:S(2)}, u32[]{:S(2)}) collective-permute-start(bf16[128,512]{1,0:T(8,128)(2,1)S(1)} %constant_dynamic-slice_fusion), channel_id=1, source_target_pairs={{0,4},{4,0},{1,5},{5,1},{2,6},{6,2},{3,7},{7,3},{8,12},{12,8},{9,1... | collective-permute-start | bytes 393224 | tf_op jit(solution)/shard_map/ppermute | solution.py:26
  9.3 3.6 %collective-permute-start.3 = (f32[1,256]{1,0:T(1,128)S(1)}, f32[1,256]{1,0:T(1,128)S(1)}, u32[]{:S(2)}, u32[]{:S(2)}) collective-permute-start(f32[1,256]{1,0:T(1,128)S(1)} %bitcast.85), channel_id=1, source_target_pairs={{0,1},{1,0},{2,3},{3,2},{4,5},{5,4},{6,7},{7,6},{8,9},{9,8},{10,11... | collective-permute-start | bytes 3080 | tf_op jit(solution)/shard_map/ppermute | solution.py:26
  13.0 3.6 %collective-permute-start.5 = (f32[1,256]{1,0:T(1,128)S(1)}, f32[1,256]{1,0:T(1,128)S(1)}, u32[]{:S(2)}, u32[]{:S(2)}) collective-permute-start(f32[1,256]{1,0:T(1,128)S(1)} %bitcast.87), channel_id=1, source_target_pairs={{0,2},{1,3},{2,0},{3,1},{4,6},{5,7},{6,4},{7,5},{8,10},{9,11},{10,... | collective-permute-start | bytes 3080 | tf_op jit(solution)/shard_map/ppermute | solution.py:26
  16.5 4.5 %collective-permute-start.7 = (f32[1,256]{1,0:T(1,128)S(1)}, f32[1,256]{1,0:T(1,128)S(1)}, u32[]{:S(2)}, u32[]{:S(2)}) collective-permute-start(f32[1,256]{1,0:T(1,128)S(1)} %bitcast.88), channel_id=1, source_target_pairs={{0,3},{1,2},{2,1},{3,0},{4,7},{5,6},{6,5},{7,4},{8,11},{9,10},{10,... | collective-permute-start | bytes 3080 | tf_op jit(solution)/shard_map/ppermute | solution.py:26
  22.6 1.4 %collective-permute-start.1 = (bf16[128,512]{1,0:T(8,128)(2,1)S(1)}, bf16[128,512]{1,0:T(8,128)(2,1)S(1)}, u32[]{:S(2)}, u32[]{:S(2)}) collective-permute-start(bf16[128,512]{1,0:T(8,128)(2,1)S(1)} %collective-permute-done), channel_id=1, source_target_pairs={{0,8},{8,0},{1,9},{9,1},{2,10},{10,2},{3,11},{11,3},{4,12},{12,4},... | collective-permute-start | bytes 393224 | tf_op jit(solution)/shard_map/ppermute | solution.py:26
  25.6 4.6 %collective-permute-start.10 = (f32[1,1024]{1,0:T(1,128)S(1)}, f32[1,1024]{1,0:T(1,128)S(1)}, u32[]{:S(2)}, u32[]{:S(2)}) collective-permute-start(f32[1,1024]{1,0:T(1,128)S(1)} %constant_dynamic-update-slice_fusion), channel_id=1, source_target_pairs={{0,3},{1,2},{2,1},{3,0},{4,7},{5,6},{6,5},{7,4},{8,11},{9,10},{10,... | collective-permute-start | bytes 12296 | tf_op jit(solution)/shard_map/ppermute | solution.py:26
  28.2 3.6 %collective-permute-start.8 = (f32[1,1024]{1,0:T(1,128)S(1)}, f32[1,1024]{1,0:T(1,128)S(1)}, u32[]{:S(2)}, u32[]{:S(2)}) collective-permute-start(f32[1,1024]{1,0:T(1,128)S(1)} %constant_dynamic-update-slice_fusion), channel_id=1, source_target_pairs={{0,1},{1,0},{2,3},{3,2},{4,5},{5,4},{6,7},{7,6},{8,9},{9,8},{10,11... | collective-permute-start | bytes 12296 | tf_op jit(solution)/shard_map/ppermute | solution.py:26
  28.7 3.6 %collective-permute-start.9 = (f32[1,1024]{1,0:T(1,128)S(1)}, f32[1,1024]{1,0:T(1,128)S(1)}, u32[]{:S(2)}, u32[]{:S(2)}) collective-permute-start(f32[1,1024]{1,0:T(1,128)S(1)} %constant_dynamic-update-slice_fusion), channel_id=1, source_target_pairs={{0,2},{1,3},{2,0},{3,1},{4,6},{5,7},{6,4},{7,5},{8,10},{9,11},{10,... | collective-permute-start | bytes 12296 | tf_op jit(solution)/shard_map/ppermute | solution.py:26
  33.8 1.6 %collective-permute-start.15 = (bf16[256,512]{1,0:T(8,128)(2,1)S(1)}, bf16[256,512]{1,0:T(8,128)(2,1)S(1)}, u32[]{:S(2)}, u32[]{:S(2)}) collective-permute-start(bf16[256,512]{1,0:T(8,128)(2,1)S(1)} %convolution_convert_fusion), channel_id=1, source_target_pairs={{0,8},{8,0},{1,9},{9,1},{2,10},{10,2},{3,11},{11,3},{4,12},{12,4},... | collective-permute-start | bytes 786440 | tf_op jit(solution)/shard_map/ppermute | solution.py:26
  35.5 4.3 %collective-permute-start.16 = (bf16[64,512]{1,0:T(8,128)(2,1)S(1)}, bf16[64,512]{1,0:T(8,128)(2,1)S(1)}, u32[]{:S(2)}, u32[]{:S(2)}) collective-permute-start(bf16[64,512]{1,0:T(8,128)(2,1)S(1)} %get-tuple-element.21), channel_id=1, source_target_pairs={{0,1},{1,0},{16,17},{17,16},{2,3},{3,2},{18,19},{19,18},{4,5},{5,4... | collective-permute-start | bytes 196616 | tf_op jit(solution)/shard_map/ppermute | solution.py:26
  37.1 4.9 %collective-permute-start.17 = (bf16[64,512]{1,0:T(8,128)(2,1)S(1)}, bf16[64,512]{1,0:T(8,128)(2,1)S(1)}, u32[]{:S(2)}, u32[]{:S(2)}) collective-permute-start(bf16[64,512]{1,0:T(8,128)(2,1)S(1)} %get-tuple-element.23), channel_id=1, source_target_pairs={{0,16},{1,17},{16,0},{17,1},{2,18},{3,19},{18,2},{19,3},{4,20},{5,... | collective-permute-start | bytes 196616 | tf_op jit(solution)/shard_map/ppermute | solution.py:26
  38.6 5.2 %collective-permute-start.18 = (bf16[64,512]{1,0:T(8,128)(2,1)S(1)}, bf16[64,512]{1,0:T(8,128)(2,1)S(1)}, u32[]{:S(2)}, u32[]{:S(2)}) collective-permute-start(bf16[64,512]{1,0:T(8,128)(2,1)S(1)} %get-tuple-element.22), channel_id=1, source_target_pairs={{0,17},{1,16},{16,1},{17,0},{2,19},{3,18},{18,3},{19,2},{4,21},{5,... | collective-permute-start | bytes 196616 | tf_op jit(solution)/shard_map/ppermute | solution.py:26
  39.4 8.9 %collective-permute-start.11 = (bf16[256,512]{1,0:T(8,128)(2,1)S(1)}, bf16[256,512]{1,0:T(8,128)(2,1)S(1)}, u32[]{:S(2)}, u32[]{:S(2)}) collective-permute-start(bf16[256,512]{1,0:T(8,128)(2,1)S(1)} %fusion), channel_id=1, source_target_pairs={{0,8},{8,0},{1,9},{9,1},{2,10},{10,2},{3,11},{11,3},{4,12},{12,4},... | collective-permute-start | bytes 786440 | tf_op jit(solution)/shard_map/ppermute | solution.py:26
  43.8 10.3 %collective-permute-start.19 = (bf16[64,512]{1,0:T(8,128)(2,1)S(1)}, bf16[64,512]{1,0:T(8,128)(2,1)S(1)}, u32[]{:S(2)}, u32[]{:S(2)}) collective-permute-start(bf16[64,512]{1,0:T(8,128)(2,1)S(1)} %add_convert_fusion.1), channel_id=1, source_target_pairs={{0,4},{2,6},{4,0},{6,2},{1,5},{3,7},{5,1},{7,3},{8,12},{10,14},{12... | collective-permute-start | bytes 196616 | tf_op jit(solution)/shard_map/ppermute | solution.py:26
  44.2 9.9 %collective-permute-start.20 = (bf16[64,512]{1,0:T(8,128)(2,1)S(1)}, bf16[64,512]{1,0:T(8,128)(2,1)S(1)}, u32[]{:S(2)}, u32[]{:S(2)}) collective-permute-start(bf16[64,512]{1,0:T(8,128)(2,1)S(1)} %add_convert_fusion.1), channel_id=1, source_target_pairs={{0,2},{2,0},{4,6},{6,4},{1,3},{3,1},{5,7},{7,5},{8,10},{10,8},{12,... | collective-permute-start | bytes 196616 | tf_op jit(solution)/shard_map/ppermute | solution.py:26
  44.8 9.2 %collective-permute-start.21 = (bf16[64,512]{1,0:T(8,128)(2,1)S(1)}, bf16[64,512]{1,0:T(8,128)(2,1)S(1)}, u32[]{:S(2)}, u32[]{:S(2)}) collective-permute-start(bf16[64,512]{1,0:T(8,128)(2,1)S(1)} %add_convert_fusion.1), channel_id=1, source_target_pairs={{0,6},{2,4},{4,2},{6,0},{1,7},{3,5},{5,3},{7,1},{8,14},{10,12},{12... | collective-permute-start | bytes 196616 | tf_op jit(solution)/shard_map/ppermute | solution.py:26
  48.6 9.1 %collective-permute-start.12 = (bf16[128,512]{1,0:T(8,128)(2,1)S(1)}, bf16[128,512]{1,0:T(8,128)(2,1)S(1)}, u32[]{:S(2)}, u32[]{:S(2)}) collective-permute-start(bf16[128,512]{1,0:T(8,128)(2,1)S(1)} %slice.181), channel_id=1, source_target_pairs={{0,4},{4,0},{1,5},{5,1},{2,6},{6,2},{3,7},{7,3},{8,12},{12,8},{9,1... | collective-permute-start | bytes 393224 | tf_op jit(solution)/shard_map/ppermute | solution.py:26
  54.1 4.6 %collective-permute-start.22 = (bf16[64,512]{1,0:T(8,128)(2,1)S(1)}, bf16[64,512]{1,0:T(8,128)(2,1)S(1)}, u32[]{:S(2)}, u32[]{:S(2)}) collective-permute-start(bf16[64,512]{1,0:T(8,128)(2,1)S(1)} %get-tuple-element.18), channel_id=1, source_target_pairs={{0,1},{1,0},{16,17},{17,16},{2,3},{3,2},{18,19},{19,18},{4,5},{5,4... | collective-permute-start | bytes 196616 | tf_op jit(solution)/shard_map/ppermute | solution.py:26
  55.2 5.0 %collective-permute-start.23 = (bf16[64,512]{1,0:T(8,128)(2,1)S(1)}, bf16[64,512]{1,0:T(8,128)(2,1)S(1)}, u32[]{:S(2)}, u32[]{:S(2)}) collective-permute-start(bf16[64,512]{1,0:T(8,128)(2,1)S(1)} %get-tuple-element.18), channel_id=1, source_target_pairs={{0,16},{1,17},{16,0},{17,1},{2,18},{3,19},{18,2},{19,3},{4,20},{5,... | collective-permute-start | bytes 196616 | tf_op jit(solution)/shard_map/ppermute | solution.py:26
  56.0 5.9 %collective-permute-start.24 = (bf16[64,512]{1,0:T(8,128)(2,1)S(1)}, bf16[64,512]{1,0:T(8,128)(2,1)S(1)}, u32[]{:S(2)}, u32[]{:S(2)}) collective-permute-start(bf16[64,512]{1,0:T(8,128)(2,1)S(1)} %get-tuple-element.18), channel_id=1, source_target_pairs={{0,17},{1,16},{16,1},{17,0},{2,19},{3,18},{18,3},{19,2},{4,21},{5,... | collective-permute-start | bytes 196616 | tf_op jit(solution)/shard_map/ppermute | solution.py:26
  57.7 5.0 %collective-permute-start.13 = (bf16[128,512]{1,0:T(8,128)(2,1)S(1)}, bf16[128,512]{1,0:T(8,128)(2,1)S(1)}, u32[]{:S(2)}, u32[]{:S(2)}) collective-permute-start(bf16[128,512]{1,0:T(8,128)(2,1)S(1)} %fusion.27), channel_id=1, source_target_pairs={{0,16},{16,0},{1,17},{17,1},{2,18},{18,2},{3,19},{19,3},{4,20},{20... | collective-permute-start | bytes 393224 | tf_op jit(solution)/shard_map/ppermute | solution.py:26
  61.9 1.8 %collective-permute-start.25 = (bf16[256,512]{1,0:T(8,128)(2,1)S(1)}, bf16[256,512]{1,0:T(8,128)(2,1)S(1)}, u32[]{:S(2)}, u32[]{:S(2)}) collective-permute-start(bf16[256,512]{1,0:T(8,128)(2,1)S(1)} %constant_dynamic-update-slice_fusion.14), channel_id=1, source_target_pairs={{0,8},{8,0},{1,9},{9,1},{2,10},{10,2},{3,11},{11,3},{4,12},{12,4},... | collective-permute-start | bytes 786440 | tf_op jit(solution)/shard_map/ppermute | solution.py:26
  63.1 1.8 %collective-permute-start.14 = (f32[128,512]{1,0:T(8,128)S(1)}, f32[128,512]{1,0:T(8,128)S(1)}, u32[]{:S(2)}, u32[]{:S(2)}) collective-permute-start(f32[128,512]{1,0:T(8,128)S(1)} %get-tuple-element.20), channel_id=1, source_target_pairs={{0,8},{8,0},{1,9},{9,1},{2,10},{10,2},{3,11},{11,3},{4,12},{12,4},... | collective-permute-start | bytes 786440 | tf_op jit(solution)/shard_map/ppermute | solution.py:26
  65.0 0.8 %copy-start.3 = (f32[256,512]{1,0:T(8,128)}, f32[256,512]{1,0:T(8,128)S(1)}, u32[]{:S(2)}) copy-start(f32[256,512]{1,0:T(8,128)S(1)} %constant_dynamic-update-slice_fusion.18) | copy-start | bytes 1572868
where the time goes:
time: 65.9 us; the launch traced here: 65.7 us
  starting transfers between devices  29.9 us (45%)
  waiting for transfers between devices  24.3 us (37%)
  matrix products  4.34 us (7%)
  other arithmetic  3.78 us (6%)
  local copies, waits for them, and re-layouts  2.14 us (3%)
  between operations  1.21 us (2%)
    ppermute x26, starting transfers between devices, swap(): return lax.ppermute(x, axes, [(i, i ^ mask) for i in range(size_of(axes))])  29.9 us
    ppermute x26, waiting for transfers between devices, swap(): return lax.ppermute(x, axes, [(i, i ^ mask) for i in range(size_of(axes))])  24.3 us
    dot_general x13, matrix products, dot(): lax.dot_general(a, b, (((ca,), (cb,)), ((), ())), preferred_element_type=...  4.34 us
  transfers between devices with their start and end apart: 26, of which 15 were waited for; matrix products, arithmetic and copies ran while one was open for 9% of the time, Pallas kernels for 0%

commit v1 on v0

--- a/solution.py
+++ b/solution.py
@@ -78,46 +78,40 @@
     c_dev = centers.shape[0]
     half = c_dev // nl
     at_s, at_k, at_l = (lax.axis_index(a) for a in (s_axes, "k", "dl"))
-    mine = lax.optimization_barrier(lax.dynamic_slice_in_dim(centers, at_l * half, half))
-    own_parts = [mine] + [swap(mine, ("k",), j) for j in range(1, nk)]
+    split = lax.optimization_barrier(
+        tuple(lax.dynamic_slice_in_dim(centers, (at_l ^ c) * half, half) for c in range(nl))
+    )
+    own_parts = [split[0]] + [swap(split[0], ("k",), j) for j in range(1, nk)]
     blocks = [pooled] + [swap(pooled, s_axes, m) for m in range(1, ns)]
     meta = lax.optimization_barrier(jnp.concatenate([labels.astype(F32), row_weight.astype(F32)]).reshape(1, 2 * rows))
     metas = [meta] + [swap(meta, s_axes, m) for m in range(1, ns)]
-    label_of = [m[:, :rows].astype(jnp.int32) for m in metas]
-    weights = [m[:, rows:] for m in metas]
     cents = list(own_parts)
     for c in range(1, nl):
-        cents.append(lax.dynamic_slice_in_dim(centers, (at_l ^ c) * half, half))
+        cents.append(split[c])
         cents += [swap(own_parts[j], ("dl",), c) for j in range(1, nk)]
     pairs = [unit_rows(part.astype(F32)) for part in cents]
     unit = jnp.concatenate([p[0] for p in pairs], axis=0)
     c_inv = pairs[0][1]
-    label_all = jnp.concatenate(label_of, axis=1)
-    weight_all = jnp.concatenate(weights, axis=1)
+    label_all = jnp.concatenate([m[:, :rows] for m in metas], axis=1).astype(jnp.int32)
+    weight_all = jnp.concatenate([m[:, rows:] for m in metas], axis=1)
     local = lax.broadcasted_iota(jnp.int32, (half, 1), 0)
     ids = jnp.concatenate(
         [local + ((at_k ^ j) * ns + at_s) * c_dev + (at_l ^ c) * half for c in range(nl) for j in range(nk)], axis=0
     )
-    embs, z_invs, expos, stats = [], [], [], []
-    for m in range(ns):
-        emb, z_inv = unit_rows(dot(blocks[m], proj, 1, 0))
-        onehot = (ids == label_of[m]).astype(F32)
-        logits = SCALE * dot(unit, emb, 1, 1) - SCALE * MARGIN * onehot
-        expo = jnp.exp(logits)
-        stats.append((jnp.sum(expo, axis=0, keepdims=True), jnp.sum(logits * onehot, axis=0, keepdims=True)))
-        embs.append(emb)
-        z_invs.append(z_inv)
-        expos.append(expo)
-    stats = jnp.concatenate([s[0] for s in stats] + [s[1] for s in stats], axis=1)
+    feats = jnp.concatenate(blocks, axis=0)
+    emb, z_inv = unit_rows(dot(feats, proj, 1, 0))
+    onehot = (ids == label_all).astype(F32)
+    logits = SCALE * dot(unit, emb, 1, 1) - SCALE * MARGIN * onehot
+    expo = jnp.exp(logits)
+    stats = jnp.concatenate(
+        [jnp.sum(expo, axis=0, keepdims=True), jnp.sum(logits * onehot, axis=0, keepdims=True)], axis=1
+    )
     total, target = stats[:, : ns * rows], stats[:, ns * rows : ns * rows + rows]
     for m in range(1, ns):
         other = swap(stats, s_axes, m)
         total = total + jnp.concatenate([other[:, (b ^ m) * rows : ((b ^ m) + 1) * rows] for b in range(ns)], axis=1)
         target = target + other[:, (ns + m) * rows : (ns + m + 1) * rows]
     row_loss = (jnp.log(total[:, :rows]) - target).reshape(rows)
-    feats, emb, z_inv = (jnp.concatenate(x, axis=0) for x in (blocks, embs, z_invs))
-    expo = jnp.concatenate(expos, axis=1)
-    onehot = (ids == label_all).astype(F32)
     grad = (weight_all * (expo / total - onehot)).astype(BF16)
     grad_emb = SCALE * dot(grad, unit, 0, 0)
     emb_f = emb.astype(F32)
@@ -145,8 +139,11 @@
     piece = scatter_sum(piece, first)
     piece = full_sum(piece, second)
     piece = piece.astype(BF16)
-    proj_grad = gather_rows(gather_rows(piece, first), ("dl",)).astype(F32)
-
+    mine = gather_rows(piece, first)
+    others = [swap(mine, ("dl",), c) for c in range(1, nl)]
+    proj_grad = lax.optimization_barrier(jnp.concatenate([mine] * nl, axis=0).astype(F32))
+    for c, other in enumerate(others, 1):
+        proj_grad = lax.dynamic_update_slice_in_dim(proj_grad, other.astype(F32), (at_l ^ c) * cols, 0)
     return (row_loss, center_grad, proj_grad)
 
 

time: 65.9 us -> 64.5 us (0.979)
  waiting for transfers between devices: 24.3 us -> 26.3 us
  starting transfers between devices: 29.9 us -> 28.3 us
  matrix products: 4.34 us -> 3.16 us
    ppermute x26, waiting for transfers between devices: 24.3 us -> 26.3 us  [swap(): return lax.ppermute(x, axes, [(i, i ^ mask) for i in range(size_of(axes))])]
    ppermute x26, starting transfers between devices: 29.9 us -> 28.3 us  [swap(): return lax.ppermute(x, axes, [(i, i ^ mask) for i in range(size_of(axes))])]
    dot_general x13 -> x7, matrix products: 4.34 us -> 3.16 us  [dot(): lax.dot_general(a, b, (((ca,), (cb,)), ((), ())), preferred_element_type=...]
    convert_element_type x1 -> x2, other arithmetic: 1.1 us -> 0.12 us  [the longest x1 0.11 us: on_device(): jnp.concatenate([mine] * nl, axis=0).astype(F32)]
    convert_element_type x1, other arithmetic: 0.01 us -> 0.72 us  [on_device(): labels.astype(F32)]
  transfers between devices with their start and end apart: 26 -> 26, of which waited for: 15 -> 17; matrix products, arithmetic and copies ran while one was open for 9% -> 5% of each run, Pallas kernels for 0% -> 0%
where the time goes in v1:
time: 64.5 us; the launch traced here: 64.3 us
  starting transfers between devices  28.3 us (44%)
  waiting for transfers between devices  26.3 us (41%)
  other arithmetic  3.41 us (5%)
  matrix products  3.16 us (5%)
  local copies, waits for them, and re-layouts  2.06 us (3%)
  between operations  1.09 us (2%)
    ppermute x26, starting transfers between devices, swap(): return lax.ppermute(x, axes, [(i, i ^ mask) for i in range(size_of(axes))])  28.3 us
    ppermute x26, waiting for transfers between devices, swap(): return lax.ppermute(x, axes, [(i, i ^ mask) for i in range(size_of(axes))])  26.3 us
    dot_general x7, matrix products, dot(): lax.dot_general(a, b, (((ca,), (cb,)), ((), ())), preferred_element_type=...  3.16 us
  transfers between devices with their start and end apart: 26, of which 17 were waited for; matrix products, arithmetic and copies ran while one was open for 5% of the time, Pallas kernels for 0%

profile of v1, /device:TPU:0, one launch (start us, length us, event | category | flops | bytes accessed | tf_op | source)
XLA Modules:
  0.0 64.3 jit_solution(3234255448872132563)
XLA Ops:
  0.7 0.7 %convert_element_type.132 = f32[128]{0:T(128)S(1)} convert(s32[128]{0:T(128)} %param.8) | non-fusion elementwise | flops 128 | bytes 1024 | tf_op jit(solution)/shard_map/convert_element_type | solution.py:86
  1.4 3.1 %collective-permute-start.5 = (f32[1,256]{1,0:T(1,128)S(1)}, f32[1,256]{1,0:T(1,128)S(1)}, u32[]{:S(2)}, u32[]{:S(2)}) collective-permute-start(f32[1,256]{1,0:T(1,128)S(1)} %bitcast.48), channel_id=1, source_target_pairs={{0,1},{1,0},{2,3},{3,2},{4,5},{5,4},{6,7},{7,6},{8,9},{9,8},{10,11... | collective-permute-start | bytes 3080 | tf_op jit(solution)/shard_map/ppermute | solution.py:26
  4.5 1.6 %collective-permute-start.6 = (f32[1,256]{1,0:T(1,128)S(1)}, f32[1,256]{1,0:T(1,128)S(1)}, u32[]{:S(2)}, u32[]{:S(2)}) collective-permute-start(f32[1,256]{1,0:T(1,128)S(1)} %bitcast.49), channel_id=1, source_target_pairs={{0,2},{1,3},{2,0},{3,1},{4,6},{5,7},{6,4},{7,5},{8,10},{9,11},{10,... | collective-permute-start | bytes 3080 | tf_op jit(solution)/shard_map/ppermute | solution.py:26
  6.0 1.0 %constant_dynamic-slice_fusion = (bf16[128,512]{1,0:T(8,128)(2,1)S(1)}, bf16[128,512]{1,0:T(8,128)(2,1)S(1)}) fusion(bf16[256,512]{1,0:T(8,128)(2,1)} %param.7, s32[]{:T(128)S(6)} %select_n.32, s32[]{:T(128)S(6)} %select_n.31), kind=kLoop, calls=%fused_computation.76 | loop fusion | bytes 524296 | tf_op jit(solution)/shard_map/dynamic_slice | solution.py:82
  7.1 3.0 %collective-permute-start = (bf16[128,512]{1,0:T(8,128)(2,1)S(1)}, bf16[128,512]{1,0:T(8,128)(2,1)S(1)}, u32[]{:S(2)}, u32[]{:S(2)}) collective-permute-start(bf16[128,512]{1,0:T(8,128)(2,1)S(1)} %get-tuple-element.5), channel_id=1, source_target_pairs={{0,4},{4,0},{1,5},{5,1},{2,6},{6,2},{3,7},{7,3},{8,12},{12,8},{9,1... | collective-permute-start | bytes 393224 | tf_op jit(solution)/shard_map/ppermute | solution.py:26
  10.1 1.5 %collective-permute-start.2 = (bf16[128,512]{1,0:T(8,128)(2,1)S(1)}, bf16[128,512]{1,0:T(8,128)(2,1)S(1)}, u32[]{:S(2)}, u32[]{:S(2)}) collective-permute-start(bf16[128,512]{1,0:T(8,128)(2,1)S(1)} %copy-done.3), channel_id=1, source_target_pairs={{0,1},{1,0},{2,3},{3,2},{4,5},{5,4},{6,7},{7,6},{8,9},{9,8},{10,11... | collective-permute-start | bytes 393224 | tf_op jit(solution)/shard_map/ppermute | solution.py:26
  12.0 1.6 %collective-permute-start.3 = (bf16[128,512]{1,0:T(8,128)(2,1)S(1)}, bf16[128,512]{1,0:T(8,128)(2,1)S(1)}, u32[]{:S(2)}, u32[]{:S(2)}) collective-permute-start(bf16[128,512]{1,0:T(8,128)(2,1)S(1)} %copy-done.3), channel_id=1, source_target_pairs={{0,2},{1,3},{2,0},{3,1},{4,6},{5,7},{6,4},{7,5},{8,10},{9,11},{10,... | collective-permute-start | bytes 393224 | tf_op jit(solution)/shard_map/ppermute | solution.py:26
  14.1 1.2 %collective-permute-done = bf16[128,512]{1,0:T(8,128)(2,1)S(1)} collective-permute-done((bf16[128,512]{1,0:T(8,128)(2,1)S(1)}, bf16[128,512]{1,0:T(8,128)(2,1)S(1)}, u32[]{:S(2)}, u32[]{:S(2)}) %collective-permute-start) | collective-permute-done | bytes 131104 | tf_op jit(solution)/shard_map/ppermute | solution.py:26
  15.5 3.0 %collective-permute-done.3 = bf16[128,512]{1,0:T(8,128)(2,1)S(1)} collective-permute-done((bf16[128,512]{1,0:T(8,128)(2,1)S(1)}, bf16[128,512]{1,0:T(8,128)(2,1)S(1)}, u32[]{:S(2)}, u32[]{:S(2)}) %collective-permute-start.3) | collective-permute-done | bytes 131104 | tf_op jit(solution)/shard_map/ppermute | solution.py:26
  18.5 1.9 %collective-permute-done.4 = bf16[128,512]{1,0:T(8,128)(2,1)S(1)} collective-permute-done((bf16[128,512]{1,0:T(8,128)(2,1)S(1)}, bf16[128,512]{1,0:T(8,128)(2,1)S(1)}, u32[]{:S(2)}, u32[]{:S(2)}) %collective-permute-start.4) | collective-permute-done | bytes 131104 | tf_op jit(solution)/shard_map/ppermute | solution.py:26
  21.2 1.2 %collective-permute-done.1 = bf16[128,512]{1,0:T(8,128)(2,1)S(1)} collective-permute-done((bf16[128,512]{1,0:T(8,128)(2,1)S(1)}, bf16[128,512]{1,0:T(8,128)(2,1)S(1)}, u32[]{:S(2)}, u32[]{:S(2)}) %collective-permute-start.1) | collective-permute-done | bytes 131104 | tf_op jit(solution)/shard_map/ppermute | solution.py:26
  22.7 0.8 %exponential_reduce_fusion = (f32[512]{0:T(512)S(1)}, f32[512]{0:T(512)S(1)}, f32[512,512]{0,1:T(8,128)S(1)}) fusion(s32[512]{0:T(512)S(1)} %maximum_convert_fusion.1, s32[512]{0:T(512)S(1)} %bitcast.45, bf16[512,512]{0,1:T(8,128)(2,1)S(1)} %multiply_convert_fusion, bf16[128,512]{1,0:T(8,128)(2,1)S(1)} %fusion.17, bf16[128,512]{1,0:T(8,128)(2,1)S(1)} %fusion.15, ...), kind=kOutput, calls=%fused_computation.22 | convolution fusion | flops 272366592 | bytes 2105344 | tf_op jit(solution)/shard_map/dot_general | solution.py:30
  23.5 1.3 %collective-permute-start.9 = (f32[1,1024]{1,0:T(1,128)S(1)}, f32[1,1024]{1,0:T(1,128)S(1)}, u32[]{:S(2)}, u32[]{:S(2)}) collective-permute-start(f32[1,1024]{1,0:T(1,128)S(1)} %pad_maximum_fusion.3), channel_id=1, source_target_pairs={{0,2},{1,3},{2,0},{3,1},{4,6},{5,7},{6,4},{7,5},{8,10},{9,11},{10,... | collective-permute-start | bytes 12296 | tf_op jit(solution)/shard_map/ppermute | solution.py:26
  25.4 1.7 %collective-permute-start.10 = (f32[1,1024]{1,0:T(1,128)S(1)}, f32[1,1024]{1,0:T(1,128)S(1)}, u32[]{:S(2)}, u32[]{:S(2)}) collective-permute-start(f32[1,1024]{1,0:T(1,128)S(1)} %pad_maximum_fusion.3), channel_id=1, source_target_pairs={{0,3},{1,2},{2,1},{3,0},{4,7},{5,6},{6,5},{7,4},{8,11},{9,10},{10,... | collective-permute-start | bytes 12296 | tf_op jit(solution)/shard_map/ppermute | solution.py:26
  27.1 1.3 %collective-permute-done.8 = f32[1,1024]{1,0:T(1,128)S(1)} collective-permute-done((f32[1,1024]{1,0:T(1,128)S(1)}, f32[1,1024]{1,0:T(1,128)S(1)}, u32[]{:S(2)}, u32[]{:S(2)}) %collective-permute-start.8) | collective-permute-done | bytes 4128 | tf_op jit(solution)/shard_map/ppermute | solution.py:26
  28.4 1.4 %collective-permute-done.10 = f32[1,1024]{1,0:T(1,128)S(1)} collective-permute-done((f32[1,1024]{1,0:T(1,128)S(1)}, f32[1,1024]{1,0:T(1,128)S(1)}, u32[]{:S(2)}, u32[]{:S(2)}) %collective-permute-start.10) | collective-permute-done | bytes 4128 | tf_op jit(solution)/shard_map/ppermute | solution.py:26
  32.3 1.1 %collective-permute-done.15 = bf16[256,512]{1,0:T(8,128)(2,1)S(1)} collective-permute-done((bf16[256,512]{1,0:T(8,128)(2,1)S(1)}, bf16[256,512]{1,0:T(8,128)(2,1)S(1)}, u32[]{:S(2)}, u32[]{:S(2)}) %collective-permute-start.15) | collective-permute-done | bytes 262176 | tf_op jit(solution)/shard_map/ppermute | solution.py:26
  33.6 1.5 %collective-permute-start.16 = (bf16[64,512]{1,0:T(8,128)(2,1)S(1)}, bf16[64,512]{1,0:T(8,128)(2,1)S(1)}, u32[]{:S(2)}, u32[]{:S(2)}) collective-permute-start(bf16[64,512]{1,0:T(8,128)(2,1)S(1)} %get-tuple-element.13), channel_id=1, source_target_pairs={{0,1},{1,0},{16,17},{17,16},{2,3},{3,2},{18,19},{19,18},{4,5},{5,4... | collective-permute-start | bytes 196616 | tf_op jit(solution)/shard_map/ppermute | solution.py:26
  35.1 1.5 %collective-permute-start.17 = (bf16[64,512]{1,0:T(8,128)(2,1)S(1)}, bf16[64,512]{1,0:T(8,128)(2,1)S(1)}, u32[]{:S(2)}, u32[]{:S(2)}) collective-permute-start(bf16[64,512]{1,0:T(8,128)(2,1)S(1)} %get-tuple-element.15), channel_id=1, source_target_pairs={{0,16},{1,17},{16,0},{17,1},{2,18},{3,19},{18,2},{19,3},{4,20},{5,... | collective-permute-start | bytes 196616 | tf_op jit(solution)/shard_map/ppermute | solution.py:26
  37.9 2.1 %collective-permute-done.17 = bf16[64,512]{1,0:T(8,128)(2,1)S(1)} collective-permute-done((bf16[64,512]{1,0:T(8,128)(2,1)S(1)}, bf16[64,512]{1,0:T(8,128)(2,1)S(1)}, u32[]{:S(2)}, u32[]{:S(2)}) %collective-permute-start.17) | collective-permute-done | bytes 65568 | tf_op jit(solution)/shard_map/ppermute | solution.py:26
  40.0 1.8 %collective-permute-done.18 = bf16[64,512]{1,0:T(8,128)(2,1)S(1)} collective-permute-done((bf16[64,512]{1,0:T(8,128)(2,1)S(1)}, bf16[64,512]{1,0:T(8,128)(2,1)S(1)}, u32[]{:S(2)}, u32[]{:S(2)}) %collective-permute-start.18) | collective-permute-done | bytes 65568 | tf_op jit(solution)/shard_map/ppermute | solution.py:26
  41.8 1.9 %collective-permute-start.19 = (bf16[64,512]{1,0:T(8,128)(2,1)S(1)}, bf16[64,512]{1,0:T(8,128)(2,1)S(1)}, u32[]{:S(2)}, u32[]{:S(2)}) collective-permute-start(bf16[64,512]{1,0:T(8,128)(2,1)S(1)} %add_convert_fusion.1), channel_id=1, source_target_pairs={{0,4},{2,6},{4,0},{6,2},{1,5},{3,7},{5,1},{7,3},{8,12},{10,14},{12... | collective-permute-start | bytes 196616 | tf_op jit(solution)/shard_map/ppermute | solution.py:26
  43.8 2.5 %collective-permute-start.21 = (bf16[64,512]{1,0:T(8,128)(2,1)S(1)}, bf16[64,512]{1,0:T(8,128)(2,1)S(1)}, u32[]{:S(2)}, u32[]{:S(2)}) collective-permute-start(bf16[64,512]{1,0:T(8,128)(2,1)S(1)} %add_convert_fusion.1), channel_id=1, source_target_pairs={{0,6},{2,4},{4,2},{6,0},{1,7},{3,5},{5,3},{7,1},{8,14},{10,12},{12... | collective-permute-start | bytes 196616 | tf_op jit(solution)/shard_map/ppermute | solution.py:26
  46.7 1.0 %collective-permute-start.12 = (bf16[128,512]{1,0:T(8,128)(2,1)S(1)}, bf16[128,512]{1,0:T(8,128)(2,1)S(1)}, u32[]{:S(2)}, u32[]{:S(2)}) collective-permute-start(bf16[128,512]{1,0:T(8,128)(2,1)S(1)} %slice.185), channel_id=1, source_target_pairs={{0,4},{4,0},{1,5},{5,1},{2,6},{6,2},{3,7},{7,3},{8,12},{12,8},{9,1... | collective-permute-start | bytes 393224 | tf_op jit(solution)/shard_map/ppermute | solution.py:26
  47.6 5.0 %collective-permute-done.19 = bf16[64,512]{1,0:T(8,128)(2,1)S(1)} collective-permute-done((bf16[64,512]{1,0:T(8,128)(2,1)S(1)}, bf16[64,512]{1,0:T(8,128)(2,1)S(1)}, u32[]{:S(2)}, u32[]{:S(2)}) %collective-permute-start.19) | collective-permute-done | bytes 65568 | tf_op jit(solution)/shard_map/ppermute | solution.py:26
  52.8 1.2 %collective-permute-start.23 = (bf16[64,512]{1,0:T(8,128)(2,1)S(1)}, bf16[64,512]{1,0:T(8,128)(2,1)S(1)}, u32[]{:S(2)}, u32[]{:S(2)}) collective-permute-start(bf16[64,512]{1,0:T(8,128)(2,1)S(1)} %get-tuple-element.10), channel_id=1, source_target_pairs={{0,16},{1,17},{16,0},{17,1},{2,18},{3,19},{18,2},{19,3},{4,20},{5,... | collective-permute-start | bytes 196616 | tf_op jit(solution)/shard_map/ppermute | solution.py:26
  54.1 2.2 %collective-permute-start.24 = (bf16[64,512]{1,0:T(8,128)(2,1)S(1)}, bf16[64,512]{1,0:T(8,128)(2,1)S(1)}, u32[]{:S(2)}, u32[]{:S(2)}) collective-permute-start(bf16[64,512]{1,0:T(8,128)(2,1)S(1)} %get-tuple-element.10), channel_id=1, source_target_pairs={{0,17},{1,16},{16,1},{17,0},{2,19},{3,18},{18,3},{19,2},{4,21},{5,... | collective-permute-start | bytes 196616 | tf_op jit(solution)/shard_map/ppermute | solution.py:26
  56.3 0.6 collective-permute-start.13
  57.2 3.0 %collective-permute-done.24 = bf16[64,512]{1,0:T(8,128)(2,1)S(1)} collective-permute-done((bf16[64,512]{1,0:T(8,128)(2,1)S(1)}, bf16[64,512]{1,0:T(8,128)(2,1)S(1)}, u32[]{:S(2)}, u32[]{:S(2)}) %collective-permute-start.24) | collective-permute-done | bytes 65568 | tf_op jit(solution)/shard_map/ppermute | solution.py:26
  60.2 1.2 %collective-permute-done.13 = bf16[128,512]{1,0:T(8,128)(2,1)S(1)} collective-permute-done((bf16[128,512]{1,0:T(8,128)(2,1)S(1)}, bf16[128,512]{1,0:T(8,128)(2,1)S(1)}, u32[]{:S(2)}, u32[]{:S(2)}) %collective-permute-start.13) | collective-permute-done | bytes 131104 | tf_op jit(solution)/shard_map/ppermute | solution.py:26
  62.2 1.3 %collective-permute-done.14 = f32[128,512]{1,0:T(8,128)S(1)} collective-permute-done((f32[128,512]{1,0:T(8,128)S(1)}, f32[128,512]{1,0:T(8,128)S(1)}, u32[]{:S(2)}, u32[]{:S(2)}) %collective-permute-start.14) | collective-permute-done | bytes 262176 | tf_op jit(solution)/shard_map/ppermute | solution.py:26
  63.5 0.8 %copy-done.2 = f32[256,512]{1,0:T(8,128)} copy-done((f32[256,512]{1,0:T(8,128)}, f32[256,512]{1,0:T(8,128)S(1)}, u32[]{:S(2)}) %copy-start.2) | copy-done | bytes 524312
  (91 shorter events, 8.0 us)
Async XLA Ops:
  0.6 19.8 %copy-start = (bf16[512,512]{1,0:T(8,128)(2,1)S(1)}, bf16[512,512]{1,0:T(8,128)(2,1)}, u32[]{:S(2)}) copy-start(bf16[512,512]{1,0:T(8,128)(2,1)} %param.6) | copy-start | bytes 1572868
  0.6 0.7 %copy-start.4 = (bf16[128]{0:T(256)(128)(2,1)S(1)}, bf16[128]{0:T(256)(128)(2,1)}, u32[]{:S(2)}) copy-start(bf16[128]{0:T(256)(128)(2,1)} %param.9) | copy-start | bytes 772
  1.4 10.6 %collective-permute-start.5 = (f32[1,256]{1,0:T(1,128)S(1)}, f32[1,256]{1,0:T(1,128)S(1)}, u32[]{:S(2)}, u32[]{:S(2)}) collective-permute-start(f32[1,256]{1,0:T(1,128)S(1)} %bitcast.48), channel_id=1, source_target_pairs={{0,1},{1,0},{2,3},{3,2},{4,5},{5,4},{6,7},{7,6},{8,9},{9,8},{10,11... | collective-permute-start | bytes 3080 | tf_op jit(solution)/shard_map/ppermute | solution.py:26
  4.5 9.2 %collective-permute-start.6 = (f32[1,256]{1,0:T(1,128)S(1)}, f32[1,256]{1,0:T(1,128)S(1)}, u32[]{:S(2)}, u32[]{:S(2)}) collective-permute-start(f32[1,256]{1,0:T(1,128)S(1)} %bitcast.49), channel_id=1, source_target_pairs={{0,2},{1,3},{2,0},{3,1},{4,6},{5,7},{6,4},{7,5},{8,10},{9,11},{10,... | collective-permute-start | bytes 3080 | tf_op jit(solution)/shard_map/ppermute | solution.py:26
  6.0 8.1 %collective-permute-start.7 = (f32[1,256]{1,0:T(1,128)S(1)}, f32[1,256]{1,0:T(1,128)S(1)}, u32[]{:S(2)}, u32[]{:S(2)}) collective-permute-start(f32[1,256]{1,0:T(1,128)S(1)} %bitcast.50), channel_id=1, source_target_pairs={{0,3},{1,2},{2,1},{3,0},{4,7},{5,6},{6,5},{7,4},{8,11},{9,10},{10,... | collective-permute-start | bytes 3080 | tf_op jit(solution)/shard_map/ppermute | solution.py:26
  6.0 4.1 %copy-start.3 = (bf16[128,512]{1,0:T(8,128)(2,1)S(1)}, bf16[128,512]{1,0:T(8,128)(2,1)}, u32[]{:S(2)}) copy-start(bf16[128,512]{1,0:T(8,128)(2,1)} %param.5) | copy-start | bytes 393220
  7.1 8.3 %collective-permute-start = (bf16[128,512]{1,0:T(8,128)(2,1)S(1)}, bf16[128,512]{1,0:T(8,128)(2,1)S(1)}, u32[]{:S(2)}, u32[]{:S(2)}) collective-permute-start(bf16[128,512]{1,0:T(8,128)(2,1)S(1)} %get-tuple-element.5), channel_id=1, source_target_pairs={{0,4},{4,0},{1,5},{5,1},{2,6},{6,2},{3,7},{7,3},{8,12},{12,8},{9,1... | collective-permute-start | bytes 393224 | tf_op jit(solution)/shard_map/ppermute | solution.py:26
  10.1 5.4 %collective-permute-start.2 = (bf16[128,512]{1,0:T(8,128)(2,1)S(1)}, bf16[128,512]{1,0:T(8,128)(2,1)S(1)}, u32[]{:S(2)}, u32[]{:S(2)}) collective-permute-start(bf16[128,512]{1,0:T(8,128)(2,1)S(1)} %copy-done.3), channel_id=1, source_target_pairs={{0,1},{1,0},{2,3},{3,2},{4,5},{5,4},{6,7},{7,6},{8,9},{9,8},{10,11... | collective-permute-start | bytes 393224 | tf_op jit(solution)/shard_map/ppermute | solution.py:26
  12.0 6.4 %collective-permute-start.3 = (bf16[128,512]{1,0:T(8,128)(2,1)S(1)}, bf16[128,512]{1,0:T(8,128)(2,1)S(1)}, u32[]{:S(2)}, u32[]{:S(2)}) collective-permute-start(bf16[128,512]{1,0:T(8,128)(2,1)S(1)} %copy-done.3), channel_id=1, source_target_pairs={{0,2},{1,3},{2,0},{3,1},{4,6},{5,7},{6,4},{7,5},{8,10},{9,11},{10,... | collective-permute-start | bytes 393224 | tf_op jit(solution)/shard_map/ppermute | solution.py:26
  13.7 6.7 %collective-permute-start.4 = (bf16[128,512]{1,0:T(8,128)(2,1)S(1)}, bf16[128,512]{1,0:T(8,128)(2,1)S(1)}, u32[]{:S(2)}, u32[]{:S(2)}) collective-permute-start(bf16[128,512]{1,0:T(8,128)(2,1)S(1)} %copy-done.3), channel_id=1, source_target_pairs={{0,3},{1,2},{2,1},{3,0},{4,7},{5,6},{6,5},{7,4},{8,11},{9,10},{10,... | collective-permute-start | bytes 393224 | tf_op jit(solution)/shard_map/ppermute | solution.py:26
  21.1 1.4 %collective-permute-start.1 = (bf16[128,512]{1,0:T(8,128)(2,1)S(1)}, bf16[128,512]{1,0:T(8,128)(2,1)S(1)}, u32[]{:S(2)}, u32[]{:S(2)}) collective-permute-start(bf16[128,512]{1,0:T(8,128)(2,1)S(1)} %collective-permute-done), channel_id=1, source_target_pairs={{0,8},{8,0},{1,9},{9,1},{2,10},{10,2},{3,11},{11,3},{4,12},{12,4},... | collective-permute-start | bytes 393224 | tf_op jit(solution)/shard_map/ppermute | solution.py:26
  23.5 3.7 %collective-permute-start.9 = (f32[1,1024]{1,0:T(1,128)S(1)}, f32[1,1024]{1,0:T(1,128)S(1)}, u32[]{:S(2)}, u32[]{:S(2)}) collective-permute-start(f32[1,1024]{1,0:T(1,128)S(1)} %pad_maximum_fusion.3), channel_id=1, source_target_pairs={{0,2},{1,3},{2,0},{3,1},{4,6},{5,7},{6,4},{7,5},{8,10},{9,11},{10,... | collective-permute-start | bytes 12296 | tf_op jit(solution)/shard_map/ppermute | solution.py:26
  24.8 3.6 %collective-permute-start.8 = (f32[1,1024]{1,0:T(1,128)S(1)}, f32[1,1024]{1,0:T(1,128)S(1)}, u32[]{:S(2)}, u32[]{:S(2)}) collective-permute-start(f32[1,1024]{1,0:T(1,128)S(1)} %pad_maximum_fusion.3), channel_id=1, source_target_pairs={{0,1},{1,0},{2,3},{3,2},{4,5},{5,4},{6,7},{7,6},{8,9},{9,8},{10,11... | collective-permute-start | bytes 12296 | tf_op jit(solution)/shard_map/ppermute | solution.py:26
  25.4 4.5 %collective-permute-start.10 = (f32[1,1024]{1,0:T(1,128)S(1)}, f32[1,1024]{1,0:T(1,128)S(1)}, u32[]{:S(2)}, u32[]{:S(2)}) collective-permute-start(f32[1,1024]{1,0:T(1,128)S(1)} %pad_maximum_fusion.3), channel_id=1, source_target_pairs={{0,3},{1,2},{2,1},{3,0},{4,7},{5,6},{6,5},{7,4},{8,11},{9,10},{10,... | collective-permute-start | bytes 12296 | tf_op jit(solution)/shard_map/ppermute | solution.py:26
  31.9 1.6 %collective-permute-start.15 = (bf16[256,512]{1,0:T(8,128)(2,1)S(1)}, bf16[256,512]{1,0:T(8,128)(2,1)S(1)}, u32[]{:S(2)}, u32[]{:S(2)}) collective-permute-start(bf16[256,512]{1,0:T(8,128)(2,1)S(1)} %convolution_convert_fusion), channel_id=1, source_target_pairs={{0,8},{8,0},{1,9},{9,1},{2,10},{10,2},{3,11},{11,3},{4,12},{12,4},... | collective-permute-start | bytes 786440 | tf_op jit(solution)/shard_map/ppermute | solution.py:26
  33.6 4.3 %collective-permute-start.16 = (bf16[64,512]{1,0:T(8,128)(2,1)S(1)}, bf16[64,512]{1,0:T(8,128)(2,1)S(1)}, u32[]{:S(2)}, u32[]{:S(2)}) collective-permute-start(bf16[64,512]{1,0:T(8,128)(2,1)S(1)} %get-tuple-element.13), channel_id=1, source_target_pairs={{0,1},{1,0},{16,17},{17,16},{2,3},{3,2},{18,19},{19,18},{4,5},{5,4... | collective-permute-start | bytes 196616 | tf_op jit(solution)/shard_map/ppermute | solution.py:26
  35.1 4.9 %collective-permute-start.17 = (bf16[64,512]{1,0:T(8,128)(2,1)S(1)}, bf16[64,512]{1,0:T(8,128)(2,1)S(1)}, u32[]{:S(2)}, u32[]{:S(2)}) collective-permute-start(bf16[64,512]{1,0:T(8,128)(2,1)S(1)} %get-tuple-element.15), channel_id=1, source_target_pairs={{0,16},{1,17},{16,0},{17,1},{2,18},{3,19},{18,2},{19,3},{4,20},{5,... | collective-permute-start | bytes 196616 | tf_op jit(solution)/shard_map/ppermute | solution.py:26
  36.6 5.2 %collective-permute-start.18 = (bf16[64,512]{1,0:T(8,128)(2,1)S(1)}, bf16[64,512]{1,0:T(8,128)(2,1)S(1)}, u32[]{:S(2)}, u32[]{:S(2)}) collective-permute-start(bf16[64,512]{1,0:T(8,128)(2,1)S(1)} %get-tuple-element.14), channel_id=1, source_target_pairs={{0,17},{1,16},{16,1},{17,0},{2,19},{3,18},{18,3},{19,2},{4,21},{5,... | collective-permute-start | bytes 196616 | tf_op jit(solution)/shard_map/ppermute | solution.py:26
  37.5 8.8 %collective-permute-start.11 = (bf16[256,512]{1,0:T(8,128)(2,1)S(1)}, bf16[256,512]{1,0:T(8,128)(2,1)S(1)}, u32[]{:S(2)}, u32[]{:S(2)}) collective-permute-start(bf16[256,512]{1,0:T(8,128)(2,1)S(1)} %fusion.1), channel_id=1, source_target_pairs={{0,8},{8,0},{1,9},{9,1},{2,10},{10,2},{3,11},{11,3},{4,12},{12,4},... | collective-permute-start | bytes 786440 | tf_op jit(solution)/shard_map/ppermute | solution.py:26
  41.8 10.8 %collective-permute-start.19 = (bf16[64,512]{1,0:T(8,128)(2,1)S(1)}, bf16[64,512]{1,0:T(8,128)(2,1)S(1)}, u32[]{:S(2)}, u32[]{:S(2)}) collective-permute-start(bf16[64,512]{1,0:T(8,128)(2,1)S(1)} %add_convert_fusion.1), channel_id=1, source_target_pairs={{0,4},{2,6},{4,0},{6,2},{1,5},{3,7},{5,1},{7,3},{8,12},{10,14},{12... | collective-permute-start | bytes 196616 | tf_op jit(solution)/shard_map/ppermute | solution.py:26
  43.7 9.0 %collective-permute-start.20 = (bf16[64,512]{1,0:T(8,128)(2,1)S(1)}, bf16[64,512]{1,0:T(8,128)(2,1)S(1)}, u32[]{:S(2)}, u32[]{:S(2)}) collective-permute-start(bf16[64,512]{1,0:T(8,128)(2,1)S(1)} %add_convert_fusion.1), channel_id=1, source_target_pairs={{0,2},{2,0},{4,6},{6,4},{1,3},{3,1},{5,7},{7,5},{8,10},{10,8},{12,... | collective-permute-start | bytes 196616 | tf_op jit(solution)/shard_map/ppermute | solution.py:26
  43.8 8.9 %collective-permute-start.21 = (bf16[64,512]{1,0:T(8,128)(2,1)S(1)}, bf16[64,512]{1,0:T(8,128)(2,1)S(1)}, u32[]{:S(2)}, u32[]{:S(2)}) collective-permute-start(bf16[64,512]{1,0:T(8,128)(2,1)S(1)} %add_convert_fusion.1), channel_id=1, source_target_pairs={{0,6},{2,4},{4,2},{6,0},{1,7},{3,5},{5,3},{7,1},{8,14},{10,12},{12... | collective-permute-start | bytes 196616 | tf_op jit(solution)/shard_map/ppermute | solution.py:26
  46.7 9.6 %collective-permute-start.12 = (bf16[128,512]{1,0:T(8,128)(2,1)S(1)}, bf16[128,512]{1,0:T(8,128)(2,1)S(1)}, u32[]{:S(2)}, u32[]{:S(2)}) collective-permute-start(bf16[128,512]{1,0:T(8,128)(2,1)S(1)} %slice.185), channel_id=1, source_target_pairs={{0,4},{4,0},{1,5},{5,1},{2,6},{6,2},{3,7},{7,3},{8,12},{12,8},{9,1... | collective-permute-start | bytes 393224 | tf_op jit(solution)/shard_map/ppermute | solution.py:26
  52.8 4.3 %collective-permute-start.22 = (bf16[64,512]{1,0:T(8,128)(2,1)S(1)}, bf16[64,512]{1,0:T(8,128)(2,1)S(1)}, u32[]{:S(2)}, u32[]{:S(2)}) collective-permute-start(bf16[64,512]{1,0:T(8,128)(2,1)S(1)} %get-tuple-element.10), channel_id=1, source_target_pairs={{0,1},{1,0},{16,17},{17,16},{2,3},{3,2},{18,19},{19,18},{4,5},{5,4... | collective-permute-start | bytes 196616 | tf_op jit(solution)/shard_map/ppermute | solution.py:26
  52.8 4.3 %collective-permute-start.23 = (bf16[64,512]{1,0:T(8,128)(2,1)S(1)}, bf16[64,512]{1,0:T(8,128)(2,1)S(1)}, u32[]{:S(2)}, u32[]{:S(2)}) collective-permute-start(bf16[64,512]{1,0:T(8,128)(2,1)S(1)} %get-tuple-element.10), channel_id=1, source_target_pairs={{0,16},{1,17},{16,0},{17,1},{2,18},{3,19},{18,2},{19,3},{4,20},{5,... | collective-permute-start | bytes 196616 | tf_op jit(solution)/shard_map/ppermute | solution.py:26
  54.1 6.1 %collective-permute-start.24 = (bf16[64,512]{1,0:T(8,128)(2,1)S(1)}, bf16[64,512]{1,0:T(8,128)(2,1)S(1)}, u32[]{:S(2)}, u32[]{:S(2)}) collective-permute-start(bf16[64,512]{1,0:T(8,128)(2,1)S(1)} %get-tuple-element.10), channel_id=1, source_target_pairs={{0,17},{1,16},{16,1},{17,0},{2,19},{3,18},{18,3},{19,2},{4,21},{5,... | collective-permute-start | bytes 196616 | tf_op jit(solution)/shard_map/ppermute | solution.py:26
  56.3 5.1 %collective-permute-start.13 = (bf16[128,512]{1,0:T(8,128)(2,1)S(1)}, bf16[128,512]{1,0:T(8,128)(2,1)S(1)}, u32[]{:S(2)}, u32[]{:S(2)}) collective-permute-start(bf16[128,512]{1,0:T(8,128)(2,1)S(1)} %fusion.21), channel_id=1, source_target_pairs={{0,16},{16,0},{1,17},{17,1},{2,18},{18,2},{3,19},{19,3},{4,20},{20... | collective-permute-start | bytes 393224 | tf_op jit(solution)/shard_map/ppermute | solution.py:26
  60.2 1.9 %collective-permute-start.25 = (bf16[256,512]{1,0:T(8,128)(2,1)S(1)}, bf16[256,512]{1,0:T(8,128)(2,1)S(1)}, u32[]{:S(2)}, u32[]{:S(2)}) collective-permute-start(bf16[256,512]{1,0:T(8,128)(2,1)S(1)} %constant_dynamic-update-slice_fusion.4), channel_id=1, source_target_pairs={{0,8},{8,0},{1,9},{9,1},{2,10},{10,2},{3,11},{11,3},{4,12},{12,4},... | collective-permute-start | bytes 786440 | tf_op jit(solution)/shard_map/ppermute | solution.py:26
  61.9 1.6 %collective-permute-start.14 = (f32[128,512]{1,0:T(8,128)S(1)}, f32[128,512]{1,0:T(8,128)S(1)}, u32[]{:S(2)}, u32[]{:S(2)}) collective-permute-start(f32[128,512]{1,0:T(8,128)S(1)} %get-tuple-element.12), channel_id=1, source_target_pairs={{0,8},{8,0},{1,9},{9,1},{2,10},{10,2},{3,11},{11,3},{4,12},{12,4},... | collective-permute-start | bytes 786440 | tf_op jit(solution)/shard_map/ppermute | solution.py:26
  62.1 1.4 %copy-start.1 = (f32[512,512]{1,0:T(8,128)}, f32[512,512]{1,0:T(8,128)S(1)}, u32[]{:S(2)}) copy-start(f32[512,512]{1,0:T(8,128)S(1)} %convert_dynamic-update-slice_fusion) | copy-start | bytes 3145732
  63.5 0.8 %copy-start.2 = (f32[256,512]{1,0:T(8,128)}, f32[256,512]{1,0:T(8,128)S(1)}, u32[]{:S(2)}) copy-start(f32[256,512]{1,0:T(8,128)S(1)} %constant_dynamic-update-slice_fusion.8) | copy-start | bytes 1572868
